TPU v7x, 256 devices: a whole 4x4x8 slice. The times are simulated.
256 devices in a mesh: leaf: 16 (over y, x), row: 16 (over z, core).
Axes of the slice: x: 4, y: 4, z: 8, core: 2. Of those that a mesh axis runs over, the one named last changes fastest.
Arguments:
- sigma_root: float32 [2048, 2048], P(None, 'row')
- linv_one: bfloat16 [16, 2048, 2048], P('leaf', None, 'row'), as said below
- panel_one: bfloat16 [16, 512, 2048], P('leaf', None, 'row'), may hold values from -1.25 to 1.25
- tiles_one: int32 [16, 4], replicated, may hold values from 0 to 15, as said below
- mask_one: int32 [16, 4, 16], P('leaf', None, 'row'), may hold values 0 or 1
- linv_two: bfloat16 [16, 2048, 2048], P('leaf', None, 'row'), as said below
- panel_two: bfloat16 [16, 512, 2048], P('leaf', None, 'row'), may hold values from -1.25 to 1.25
- tiles_two: int32 [16, 4], replicated, may hold values from 0 to 15, as said below
- mask_two: int32 [16, 4, 16], P('leaf', None, 'row'), may hold values 0 or 1
- parent: int32 [16], replicated, may hold values from 0 to 15
Outputs:
- sigma_one: float32 [16, 2048, 2048], P('leaf', None, 'row')
- cross_one: float32 [16, 512, 2048], P('leaf', None, 'row')
- sigma_two: float32 [16, 2048, 2048], P('leaf', None, 'row')
- cross_two: float32 [16, 512, 2048], P('leaf', None, 'row')
Inputs may be any that keep to these rules, and one draw needn't show every extreme that they name: `tiles_one`: each row holds 4 different tile numbers in increasing order. `tiles_two`: each row holds 4 different tile numbers in increasing order. `linv_one`: each block is lower triangular with a positive diagonal. `sigma_root`: symmetric. `linv_two`: each block is lower triangular with a positive diagonal.
All inputs are finite; a program needn't handle non-finite values. No bound on the sum of `mask_one` or of `mask_two` on one device may be relied on, other than what follows from the above.
Results may differ from a plain program's by a relative error of at most 0.00045.
Values may be sent and summed in bfloat16 or wider, within the bound.
No kernel may reach another device: no remote copies, remote signals or barrier semaphores. Data moves between devices by JAX's collectives and lax.ppermute only.
A program may use at most 64 MiB of HBM per device.

v0:
```python
import jax
import jax.numpy as jnp
from jax import lax
from jax.sharding import PartitionSpec as P

TILE = 128


def pattern_rows(tile_list):
    offsets = jnp.arange(TILE, dtype=jnp.int32)
    return (tile_list[..., None] * TILE + offsets).reshape(tile_list.shape[:-1] + (-1,))


def expand_mask(tile_mask):
    return jnp.repeat(jnp.repeat(tile_mask, TILE, axis=0), TILE, axis=1)


def assemble(selected, row_list):
    gathered = lax.all_gather(selected, "row", axis=1, tiled=True)
    return jnp.take(gathered, row_list, axis=1)


def solve_block(selected, row_list, linv_local, panel_local, mask_local):
    select = assemble(selected, row_list)
    masked = panel_local * expand_mask(mask_local).astype(jnp.bfloat16)
    linv_wide = linv_local.astype(jnp.float32)
    whole_panel = lax.all_gather(masked, "row", axis=1, tiled=True)
    upper_part = jnp.dot(whole_panel, linv_local, preferred_element_type=jnp.float32)
    cross = -jnp.dot(select, upper_part, precision=lax.Precision.HIGHEST)
    middle = linv_wide - jnp.dot(
        whole_panel.astype(jnp.float32).T, cross, precision=lax.Precision.HIGHEST
    )
    sigma = jnp.dot(
        lax.all_gather(linv_local, "row", axis=1, tiled=True).astype(jnp.float32).T,
        middle,
        precision=lax.Precision.HIGHEST,
    )
    return (sigma, cross)


def body(
    sigma_root,
    linv_one,
    panel_one,
    tiles_one,
    mask_one,
    linv_two,
    panel_two,
    tiles_two,
    mask_two,
    parent,
):
    leaf_id = lax.axis_index("leaf")
    width = sigma_root.shape[1]
    own_tiles = lax.dynamic_index_in_dim(tiles_one, leaf_id, 0, keepdims=False)
    rows_first = pattern_rows(own_tiles)
    selected_first = jnp.take(sigma_root, rows_first, axis=0)
    sigma_first, cross_first = solve_block(
        selected_first, rows_first, linv_one[0], panel_one[0], mask_one[0]
    )
    rows_every = pattern_rows(tiles_two)
    count = rows_every.shape[0]
    block_rows = rows_every.shape[1]
    owned = (parent == leaf_id).astype(jnp.float32)
    slots = jnp.take(sigma_first, rows_every.reshape(-1), axis=0).reshape(count, block_rows, width)
    slots = slots * owned[:, None, None]
    arrived = lax.all_to_all(slots, "leaf", split_axis=0, concat_axis=0, tiled=True)
    selected_second = jnp.sum(arrived, axis=0)
    rows_second = lax.dynamic_index_in_dim(rows_every, leaf_id, 0, keepdims=False)
    sigma_second, cross_second = solve_block(
        selected_second, rows_second, linv_two[0], panel_two[0], mask_two[0]
    )
    return (sigma_first[None], cross_first[None], sigma_second[None], cross_second[None])


def solution(mesh):
    return jax.shard_map(
        body,
        mesh=mesh,
        in_specs=(
            P(None, "row"),
            P("leaf", None, "row"),
            P("leaf", None, "row"),
            P(),
            P("leaf", None, "row"),
            P("leaf", None, "row"),
            P("leaf", None, "row"),
            P(),
            P("leaf", None, "row"),
            P(),
        ),
        out_specs=(
            P("leaf", None, "row"),
            P("leaf", None, "row"),
            P("leaf", None, "row"),
            P("leaf", None, "row"),
        ),
        check_vma=False,
    )
```

profile of v0, /device:TPU:1, one launch (start us, length us, event | category | flops | bytes accessed | tf_op | source)
XLA Modules:
  0.0 404.3 jit_solution(16791441184361963141)
XLA Ops:
  7.2 0.0 copy-start
  7.2 0.0 copy-start.1
  7.2 0.0 all-gather.9.cloned.1.call-start
  7.2 0.8 convert_bitcast_fusion.1
  8.0 0.1 broadcast_bitcast_fusion.1
  8.1 1.7 bitcast_multiply_fusion.1
  9.8 0.0 all-gather.9.cloned.1.call-update
  9.8 0.0 all-gather.11.cloned.1.call-start
  9.9 0.9 multiply_reduce_fusion
  10.7 0.1 iota_add_fusion.1
  10.8 0.0 copy-done
  10.8 1.0 gather_fusion
  11.9 0.1 compare_and_fusion.2
  11.9 0.8 broadcast_select_fusion
  12.8 0.0 all-gather.11.cloned.1.call-update
  12.8 0.0 all-gather.17.cloned.1.call-start
  12.9 0.7 all-gather.17.cloned.1.call-update
  13.5 0.7 broadcast_multiply_fusion
  14.2 0.1 copy.20
  14.3 0.1 compare_select_fusion.4
  14.4 0.7 compare_convert_fusion
  15.1 0.7 convert_bitcast_fusion
  15.7 0.1 broadcast_bitcast_fusion
  15.8 0.1 iota_add_fusion
  15.9 0.1 add.146
  16.1 39.5 %all-gather.9.cloned.1.call-done = bf16[512,2048]{1,0:T(8,128)(2,1)} async-done(((bf16[512,128]{1,0:T(8,128)(2,1)}), bf16[512,2048]{1,0:T(8,128)(2,1)}) %all-gather.9.cloned.1.call-update) | async-done | bytes 2097168 | tf_op jit(solution)/shard_map/all_gather | solution.py:27
  55.5 0.0 copy-done.1
  55.5 2.3 fusion.13
  57.8 48.6 %all-gather.11.cloned.1.call-done = f32[512,2048]{1,0:T(8,128)} async-done(((f32[512,128]{1,0:T(8,128)}), f32[512,2048]{1,0:T(8,128)}) %all-gather.11.cloned.1.call-update) | async-done | bytes 4194320 | tf_op jit(solution)/shard_map/all_gather | solution.py:19
  106.5 5.3 %copy.19 = f32[512,2048]{0,1:T(8,128)} copy(f32[512,2048]{1,0:T(8,128)} %all-gather.11.cloned.1.call-done) | data formatting | bytes 8388608 | tf_op jit(solution)/shard_map/all_gather | solution.py:19
  111.8 4.2 %gather_fusion.2 = f32[512,512]{1,0:T(8,128)S(1)} fusion(f32[512,2048]{0,1:T(8,128)} %copy.19, s32[1024]{0:T(1024)S(1)} %pad_clamp_fusion.1), kind=kCustom, calls=%fused_computation.clone | custom fusion | bytes 2099200 | tf_op jit(solution)/shard_map/jit(_take)/gather | solution.py:20
  116.0 1.9 convolution_negate_fusion.1
  117.9 0.0 copy-start.4
  117.9 0.7 copy-done.4
  118.6 3.9 convolution_subtract_fusion.1
  122.6 50.3 %all-gather.17.cloned.1.call-done = bf16[1,2048,2048]{2,1,0:T(8,128)(2,1)} async-done(((bf16[1,2048,128]{2,1,0:T(8,128)(2,1)}), bf16[1,2048,2048]{2,1,0:T(8,128)(2,1)}) %all-gather.17.cloned.1.call-update) | async-done | bytes 8388624 | tf_op jit(solution)/shard_map/all_gather | solution.py:34
  172.9 6.3 %fusion.2 = f32[128,2048]{1,0:T(8,128)S(1)} fusion(f32[2048,128]{1,0:T(8,128)S(1)} %convolution_subtract_fusion.1, bf16[1,2048,2048]{2,1,0:T(8,128)(2,1)} %all-gather.17.cloned.1.call-done), kind=kOutput, calls=%fused_computation.6 | convolution fusion | flops 6442450944 | bytes 10485760 | tf_op jit(solution)/shard_map/dot_general | solution.py:33
  179.1 0.3 copy.21
  179.5 27.8 %gather_fusion.1 = f32[8192,128]{1,0:T(8,128)} fusion(f32[2048,128]{1,0:T(8,128)S(1)} %copy.21, s32[8192]{0:T(1024)S(1)} %broadcast_clamp_fusion), kind=kCustom, calls=%fused_computation.3 | custom fusion | bytes 8421376 | tf_op jit(solution)/shard_map/jit(_take)/gather | solution.py:65
  207.3 5.3 %select_multiply_fusion = f32[16,512,128]{2,1,0:T(8,128)} fusion(f32[16,512,128]{2,1,0:T(8,128)} %bitcast.84, f32[16]{0:T(128)S(1)} %compare_convert_fusion, pred[16,512]{1,0:T(8,128)(4,1)S(1)} %compare_and_fusion), kind=kLoop, calls=%fused_computation.8 | loop fusion | flops 2097152 | bytes 8396864 | tf_op jit(solution)/shard_map/mul | solution.py:66
  212.5 4.7 %all-to-all-start = ((f32[16,512,128]{2,1,0:T(8,128)}), f32[16,512,128]{2,1,0:T(8,128)}, u32[]{:S(2)}, u32[]{:S(2)}) async-start(f32[16,512,128]{2,1,0:T(8,128)} %select_multiply_fusion), calls=%async_computation | async-start | bytes 8388608 | tf_op jit(solution)/shard_map/all_to_all | solution.py:67
  217.2 0.0 copy-start.2
  217.2 0.0 all-gather.13.cloned.1.call-start
  217.3 0.0 copy-done.6
  217.3 0.8 bitcast_multiply_fusion
  218.1 0.0 all-gather.13.cloned.1.call-update
  218.1 0.0 all-gather.15.cloned.1.call-start
  218.2 62.3 %all-to-all-done = f32[16,512,128]{2,1,0:T(8,128)} async-done(((f32[16,512,128]{2,1,0:T(8,128)}), f32[16,512,128]{2,1,0:T(8,128)}, u32[]{:S(2)}, u32[]{:S(2)}) %all-to-all-start) | async-done | bytes 4194336 | tf_op jit(solution)/shard_map/all_to_all | solution.py:67
  280.5 2.4 reduce_sum.9
  282.9 0.8 copy.22
  283.7 0.0 all-gather.15.cloned.1.call-update
  283.7 0.2 all-gather.19.cloned.1.call-start
  284.0 0.3 all-gather.19.cloned.1.call-update
  284.4 0.0 all-gather.13.cloned.1.call-done
  284.4 2.3 fusion.11
  286.7 1.3 copy.23
  288.0 35.5 %all-gather.15.cloned.1.call-done = f32[512,2048]{0,1:T(8,128)} async-done(((f32[512,128]{0,1:T(8,128)}), f32[512,2048]{0,1:T(8,128)}) %all-gather.15.cloned.1.call-update) | async-done | bytes 4194320 | tf_op jit(solution)/shard_map/all_gather | solution.py:19
  323.6 4.2 %gather_fusion.3 = f32[512,512]{1,0:T(8,128)S(1)} fusion(f32[512,2048]{0,1:T(8,128)} %all-gather.15.cloned.1.call-done, s32[1024]{0:T(1024)S(1)} %pad_clamp_fusion), kind=kCustom, calls=%fused_computation.1.clone | custom fusion | bytes 2099200 | tf_op jit(solution)/shard_map/jit(_take)/gather | solution.py:20
  327.8 1.9 convolution_negate_fusion
  329.7 0.0 copy-start.5
  329.7 4.0 convolution_subtract_fusion
  333.7 56.2 %all-gather.19.cloned.1.call-done = bf16[1,2048,2048]{2,1,0:T(8,128)(2,1)} async-done(((bf16[1,2048,128]{2,1,0:T(8,128)(2,1)}), bf16[1,2048,2048]{2,1,0:T(8,128)(2,1)}) %all-gather.19.cloned.1.call-update) | async-done | bytes 8388624 | tf_op jit(solution)/shard_map/all_gather | solution.py:34
  389.9 6.3 %fusion.4 = f32[1,2048,128]{1,2,0:T(8,128)S(1)} fusion(f32[2048,128]{1,0:T(8,128)S(1)} %convolution_subtract_fusion, bf16[1,2048,2048]{2,1,0:T(8,128)(2,1)} %all-gather.19.cloned.1.call-done), kind=kOutput, calls=%fused_computation.9 | convolution fusion | flops 6442450944 | bytes 10485760 | tf_op jit(solution)/shard_map/dot_general | solution.py:33
  396.2 1.3 copy.24
  (18 shorter events, 0.1 us)
Async XLA Ops:
  7.2 3.6 copy-start
  7.2 48.4 %copy-start.1 = (bf16[1,2048,128]{2,1,0:T(8,128)(2,1)S(1)}, bf16[1,2048,128]{2,1,0:T(8,128)(2,1)}, u32[]{:S(2)}) copy-start(bf16[1,2048,128]{2,1,0:T(8,128)(2,1)} %param.13) | copy-start | bytes 1572868
  7.2 48.3 %all-gather.9.cloned.1.call-start = ((), (), s32[]{:S(2)}) async-start(), calls=%async_computation.1 | async-start | bytes 2228224 | tf_op jit(solution)/shard_map/all_gather | solution.py:27
  9.8 96.7 %all-gather.11.cloned.1.call-start = ((), (), s32[]{:S(2)}) async-start(), calls=%async_computation.2 | async-start | bytes 4456448 | tf_op jit(solution)/shard_map/all_gather | solution.py:19
  12.8 160.1 %all-gather.17.cloned.1.call-start = ((), (), s32[]{:S(2)}) async-start(), calls=%async_computation.5 | async-start | bytes 8912896 | tf_op jit(solution)/shard_map/all_gather | solution.py:34
  117.9 0.7 copy-start.4
  212.5 4.8 %copy-start.6 = (bf16[1,512,128]{2,1,0:T(8,128)(2,1)S(1)}, bf16[1,512,128]{2,1,0:T(8,128)(2,1)}, u32[]{:S(2)}) copy-start(bf16[1,512,128]{2,1,0:T(8,128)(2,1)} %param.18) | copy-start | bytes 393220
  212.5 67.9 %all-to-all-start = ((f32[16,512,128]{2,1,0:T(8,128)}), f32[16,512,128]{2,1,0:T(8,128)}, u32[]{:S(2)}, u32[]{:S(2)}) async-start(f32[16,512,128]{2,1,0:T(8,128)} %select_multiply_fusion), calls=%async_computation | async-start | bytes 8388608 | tf_op jit(solution)/shard_map/all_to_all | solution.py:67
  217.2 67.2 %copy-start.2 = (bf16[1,2048,128]{2,1,0:T(8,128)(2,1)S(1)}, bf16[1,2048,128]{2,1,0:T(8,128)(2,1)}, u32[]{:S(2)}) copy-start(bf16[1,2048,128]{2,1,0:T(8,128)(2,1)} %param.17) | copy-start | bytes 1572868
  217.2 67.2 %all-gather.13.cloned.1.call-start = ((), (), s32[]{:S(2)}) async-start(), calls=%async_computation.3 | async-start | bytes 2228224 | tf_op jit(solution)/shard_map/all_gather | solution.py:27
  218.1 105.4 %all-gather.15.cloned.1.call-start = ((), (), s32[]{:S(2)}) async-start(), calls=%async_computation.4 | async-start | bytes 4456448 | tf_op jit(solution)/shard_map/all_gather | solution.py:19
  283.7 106.2 %all-gather.19.cloned.1.call-start = ((), (), s32[]{:S(2)}) async-start(), calls=%async_computation.6 | async-start | bytes 8912896 | tf_op jit(solution)/shard_map/all_gather | solution.py:34
  288.0 41.6 %copy-start.3 = (bf16[1,2048,128]{2,1,0:T(8,128)(2,1)S(1)}, bf16[1,2048,128]{2,1,0:T(8,128)(2,1)}, u32[]{:S(2)}) copy-start(bf16[1,2048,128]{2,1,0:T(8,128)(2,1)} %param.17) | copy-start | bytes 1572868
  329.7 4.0 copy-start.5
Sparse Core Ops, SparseCore 0:
  10.4 45.1 all-gather.8
  57.9 48.5 all-gather.10
  108.2 64.6 all-gather.16
  220.1 40.0 all-gather.12
  283.9 39.6 all-gather.14
  325.2 64.6 all-gather.18
where the time goes:
time: 405 us; the launch traced here: 404 us
  waiting for transfers between devices  294 us (73%)
  local copies, waits for them, and re-layouts  47.4 us (12%)
  matrix products  28.8 us (7%)
  other arithmetic  15.1 us (4%)
  between operations  14.4 us (4%)
  starting transfers between devices  5.12 us (1%)
    all_gather x2, waiting for transfers between devices, solve_block(): lax.all_gather(linv_local, 'row', axis=1, tiled=True).astype(jnp.float32)  107 us
    all_gather x2, waiting for transfers between devices, assemble(): gathered = lax.all_gather(selected, 'row', axis=1, tiled=True)  84.1 us
    all_to_all x1, waiting for transfers between devices, body(): lax.all_to_all(slots, 'leaf', split_axis=0, concat_axis=0, tiled=True)  62.3 us
    all_gather x2, waiting for transfers between devices, solve_block(): whole_panel = lax.all_gather(masked, 'row', axis=1, tiled=True)  39.5 us
    gather x1, local copies, waits for them, and re-layouts, body(): jnp.take(sigma_first, rows_every.reshape(-1), axis=0)  27.8 us
    dot_general x2, matrix products, solve_block(): jnp.dot(lax.all_gather(linv_local, 'row', axis=1, tiled=True).astype(jnp....  12.5 us
    gather x2, local copies, waits for them, and re-layouts, assemble(): return jnp.take(gathered, row_list, axis=1)  8.43 us
  transfers between devices with their start and end apart: 7, of which 6 were waited for; matrix products, arithmetic and copies ran while one was open for 10% of the time, Pallas kernels for 0%

commit v1 on v0

--- a/solution.py
+++ b/solution.py
@@ -24,7 +24,12 @@
     select = assemble(selected, row_list)
     masked = panel_local * expand_mask(mask_local).astype(jnp.bfloat16)
     linv_wide = linv_local.astype(jnp.float32)
-    whole_panel = lax.all_gather(masked, "row", axis=1, tiled=True)
+    ring = [masked]
+    for hop in range(15):
+        ring.append(lax.ppermute(ring[-1], "row", [(dev, (dev + 1) % 16) for dev in range(16)]))
+    whole_panel = jnp.roll(
+        jnp.concatenate(ring[::-1], axis=1), (lax.axis_index("row") + 1) * ring[0].shape[1], axis=1
+    )
     upper_part = jnp.dot(whole_panel, linv_local, preferred_element_type=jnp.float32)
     cross = -jnp.dot(select, upper_part, precision=lax.Precision.HIGHEST)
     middle = linv_wide - jnp.dot(

time: 405 us -> 374 us (0.923)
  waiting for transfers between devices: 294 us -> 189 us
  blocking collectives: 0 us -> 56.9 us
  starting transfers between devices: 5.12 us -> 22.3 us
  other arithmetic: 15.1 us -> 8.87 us
    ppermute x0 -> x30, waiting for transfers between devices: none -> 179 us  [solve_block(): lax.ppermute(ring[-1], 'row', [(dev, (dev + 1) % 16) for dev in range(16)])]
    all_gather x2, waiting for transfers between devices: 107 us -> 8.76 us  [solve_block(): lax.all_gather(linv_local, 'row', axis=1, tiled=True).astype(jnp.float32)]
    all_gather x2, waiting for transfers between devices: 84.1 us -> 0.02 us  [assemble(): gathered = lax.all_gather(selected, 'row', axis=1, tiled=True)]
    all_to_all x1 -> x0, waiting for transfers between devices: 62.3 us -> none  [body(): lax.all_to_all(slots, 'leaf', split_axis=0, concat_axis=0, tiled=True)]
    all_to_all x0 -> x1, blocking collectives: none -> 56.9 us  [body(): lax.all_to_all(slots, 'leaf', split_axis=0, concat_axis=0, tiled=True)]
    all_gather x2 -> x0, waiting for transfers between devices: 39.5 us -> none  [solve_block(): whole_panel = lax.all_gather(masked, 'row', axis=1, tiled=True)]
    ppermute x0 -> x30, starting transfers between devices: none -> 22.2 us  [solve_block(): lax.ppermute(ring[-1], 'row', [(dev, (dev + 1) % 16) for dev in range(16)])]
    all_to_all x1 -> x0, starting transfers between devices: 4.69 us -> none  [body(): lax.all_to_all(slots, 'leaf', split_axis=0, concat_axis=0, tiled=True)]
  transfers between devices with their start and end apart: 7 -> 34, of which waited for: 6 -> 31; matrix products, arithmetic and copies ran while one was open for 10% -> 9% of each run, Pallas kernels for 0% -> 0%
where the time goes in v1:
time: 374 us; the launch traced here: 371 us
  waiting for transfers between devices  189 us (51%)
  blocking collectives  56.9 us (15%)
  local copies, waits for them, and re-layouts  51.4 us (14%)
  matrix products  28.2 us (8%)
  starting transfers between devices  22.3 us (6%)
  between operations  14.4 us (4%)
  other arithmetic  8.87 us (2%)
    ppermute x30, waiting for transfers between devices, solve_block(): lax.ppermute(ring[-1], 'row', [(dev, (dev + 1) % 16) for dev in range(16)])  179 us
    all_to_all x1, blocking collectives, body(): lax.all_to_all(slots, 'leaf', split_axis=0, concat_axis=0, tiled=True)  56.9 us
    gather x1, local copies, waits for them, and re-layouts, body(): jnp.take(sigma_first, rows_every.reshape(-1), axis=0)  27.9 us
    ppermute x30, starting transfers between devices, solve_block(): lax.ppermute(ring[-1], 'row', [(dev, (dev + 1) % 16) for dev in range(16)])  22.2 us
    dot_general x2, matrix products, solve_block(): jnp.dot(lax.all_gather(linv_local, 'row', axis=1, tiled=True).astype(jnp....  12.5 us
    all_gather x2, waiting for transfers between devices, solve_block(): lax.all_gather(linv_local, 'row', axis=1, tiled=True).astype(jnp.float32)  8.76 us
    dot_general x2, matrix products, solve_block(): jnp.dot(whole_panel.astype(jnp.float32).T, cross, precision=lax.Precision...  8.71 us
    gather x2, local copies, waits for them, and re-layouts, assemble(): return jnp.take(gathered, row_list, axis=1)  8.57 us
  transfers between devices with their start and end apart: 34, of which 31 were waited for; matrix products, arithmetic and copies ran while one was open for 9% of the time, Pallas kernels for 0%

profile of v1, /device:TPU:1, one launch (start us, length us, event | category | flops | bytes accessed | tf_op | source)
XLA Modules:
  0.0 370.6 jit_solution(10214467699892546171)
XLA Ops:
  7.3 0.9 multiply_reduce_fusion
  8.4 1.0 gather_fusion
  9.5 0.8 broadcast_select_fusion
  11.3 3.0 collective-permute-start
  14.4 1.9 collective-permute-done
  16.3 2.4 collective-permute-start.1
  18.8 2.9 collective-permute-done.1
  21.7 1.5 collective-permute-start.2
  23.2 4.1 %collective-permute-done.2 = bf16[512,128]{1,0:T(8,128)(2,1)S(1)} collective-permute-done((bf16[512,128]{1,0:T(8,128)(2,1)S(1)}, bf16[512,128]{1,0:T(8,128)(2,1)S(1)}, u32[]{:S(2)}, u32[]{:S(2)}) %collective-permute-start.2) | collective-permute-done | bytes 131104 | tf_op jit(solution)/shard_map/ppermute | solution.py:29
  27.6 7.3 %collective-permute-done.3 = bf16[512,128]{1,0:T(8,128)(2,1)S(1)} collective-permute-done((bf16[512,128]{1,0:T(8,128)(2,1)S(1)}, bf16[512,128]{1,0:T(8,128)(2,1)S(1)}, u32[]{:S(2)}, u32[]{:S(2)}) %collective-permute-start.3) | collective-permute-done | bytes 131104 | tf_op jit(solution)/shard_map/ppermute | solution.py:29
  34.9 6.1 %collective-permute-done.4 = bf16[512,128]{1,0:T(8,128)(2,1)S(1)} collective-permute-done((bf16[512,128]{1,0:T(8,128)(2,1)S(1)}, bf16[512,128]{1,0:T(8,128)(2,1)S(1)}, u32[]{:S(2)}, u32[]{:S(2)}) %collective-permute-start.4) | collective-permute-done | bytes 131104 | tf_op jit(solution)/shard_map/ppermute | solution.py:29
  41.0 5.7 %collective-permute-done.5 = bf16[512,128]{1,0:T(8,128)(2,1)S(1)} collective-permute-done((bf16[512,128]{1,0:T(8,128)(2,1)S(1)}, bf16[512,128]{1,0:T(8,128)(2,1)S(1)}, u32[]{:S(2)}, u32[]{:S(2)}) %collective-permute-start.5) | collective-permute-done | bytes 131104 | tf_op jit(solution)/shard_map/ppermute | solution.py:29
  46.7 6.8 %collective-permute-done.6 = bf16[512,128]{1,0:T(8,128)(2,1)S(1)} collective-permute-done((bf16[512,128]{1,0:T(8,128)(2,1)S(1)}, bf16[512,128]{1,0:T(8,128)(2,1)S(1)}, u32[]{:S(2)}, u32[]{:S(2)}) %collective-permute-start.6) | collective-permute-done | bytes 131104 | tf_op jit(solution)/shard_map/ppermute | solution.py:29
  53.5 6.2 %collective-permute-done.7 = bf16[512,128]{1,0:T(8,128)(2,1)S(1)} collective-permute-done((bf16[512,128]{1,0:T(8,128)(2,1)S(1)}, bf16[512,128]{1,0:T(8,128)(2,1)S(1)}, u32[]{:S(2)}, u32[]{:S(2)}) %collective-permute-start.7) | collective-permute-done | bytes 131104 | tf_op jit(solution)/shard_map/ppermute | solution.py:29
  60.2 6.0 %collective-permute-done.8 = bf16[512,128]{1,0:T(8,128)(2,1)S(1)} collective-permute-done((bf16[512,128]{1,0:T(8,128)(2,1)S(1)}, bf16[512,128]{1,0:T(8,128)(2,1)S(1)}, u32[]{:S(2)}, u32[]{:S(2)}) %collective-permute-start.8) | collective-permute-done | bytes 131104 | tf_op jit(solution)/shard_map/ppermute | solution.py:29
  66.3 5.5 %collective-permute-done.9 = bf16[512,128]{1,0:T(8,128)(2,1)S(1)} collective-permute-done((bf16[512,128]{1,0:T(8,128)(2,1)S(1)}, bf16[512,128]{1,0:T(8,128)(2,1)S(1)}, u32[]{:S(2)}, u32[]{:S(2)}) %collective-permute-start.9) | collective-permute-done | bytes 131104 | tf_op jit(solution)/shard_map/ppermute | solution.py:29
  71.9 5.6 %collective-permute-done.10 = bf16[512,128]{1,0:T(8,128)(2,1)S(1)} collective-permute-done((bf16[512,128]{1,0:T(8,128)(2,1)S(1)}, bf16[512,128]{1,0:T(8,128)(2,1)S(1)}, u32[]{:S(2)}, u32[]{:S(2)}) %collective-permute-start.10) | collective-permute-done | bytes 131104 | tf_op jit(solution)/shard_map/ppermute | solution.py:29
  77.5 5.5 %collective-permute-done.11 = bf16[512,128]{1,0:T(8,128)(2,1)S(1)} collective-permute-done((bf16[512,128]{1,0:T(8,128)(2,1)S(1)}, bf16[512,128]{1,0:T(8,128)(2,1)S(1)}, u32[]{:S(2)}, u32[]{:S(2)}) %collective-permute-start.11) | collective-permute-done | bytes 131104 | tf_op jit(solution)/shard_map/ppermute | solution.py:29
  83.0 8.3 %collective-permute-done.12 = bf16[512,128]{1,0:T(8,128)(2,1)S(1)} collective-permute-done((bf16[512,128]{1,0:T(8,128)(2,1)S(1)}, bf16[512,128]{1,0:T(8,128)(2,1)S(1)}, u32[]{:S(2)}, u32[]{:S(2)}) %collective-permute-start.12) | collective-permute-done | bytes 131104 | tf_op jit(solution)/shard_map/ppermute | solution.py:29
  91.4 8.2 %collective-permute-done.13 = bf16[512,128]{1,0:T(8,128)(2,1)} collective-permute-done((bf16[512,128]{1,0:T(8,128)(2,1)S(1)}, bf16[512,128]{1,0:T(8,128)(2,1)}, u32[]{:S(2)}, u32[]{:S(2)}) %collective-permute-start.13) | collective-permute-done | bytes 131104 | tf_op jit(solution)/shard_map/ppermute | solution.py:29
  99.7 8.5 %collective-permute-done.14 = bf16[512,128]{1,0:T(8,128)(2,1)} collective-permute-done((bf16[512,128]{1,0:T(8,128)(2,1)}, bf16[512,128]{1,0:T(8,128)(2,1)}, u32[]{:S(2)}, u32[]{:S(2)}) %collective-permute-start.14) | collective-permute-done | bytes 131104 | tf_op jit(solution)/shard_map/ppermute | solution.py:29
  108.2 0.9 constant_dynamic-update-slice_fusion.15
  109.1 0.9 constant_dynamic-update-slice_fusion.14
  110.9 1.3 copy-done.8
  112.2 1.2 fusion.15
  113.5 5.4 %copy.19 = f32[512,2048]{0,1:T(8,128)} copy(f32[512,2048]{1,0:T(8,128)} %all-gather.7.cloned.1.call-done) | data formatting | bytes 8388608 | tf_op jit(solution)/shard_map/all_gather | solution.py:19
  118.8 4.2 %gather_fusion.2 = f32[512,512]{1,0:T(8,128)S(1)} fusion(f32[512,2048]{0,1:T(8,128)} %copy.19, s32[1024]{0:T(1024)S(1)} %pad_clamp_fusion.1), kind=kCustom, calls=%fused_computation.clone | custom fusion | bytes 2099200 | tf_op jit(solution)/shard_map/jit(_take)/gather | solution.py:20
  123.1 1.9 convolution_negate_fusion.1
  125.0 4.3 %convolution_subtract_fusion.1 = f32[2048,128]{1,0:T(8,128)S(1)} fusion(f32[512,128]{1,0:T(8,128)S(1)} %convolution_negate_fusion.1, bf16[1,2048,128]{2,1,0:T(8,128)(2,1)S(1)} %copy-done.1, s32[]{:T(128)S(6)} %select_n.78, bf16[512,2048]{1,0:T(8,128)(2,1)} %copy-done.8), kind=kOutput, calls=%fused_computation.15 | convolution fusion | flops 1615331328 | bytes 3932164 | tf_op jit(solution)/shard_map/dot_general | solution.py:35
  129.3 8.7 %all-gather.11.cloned.1.call-done = bf16[1,2048,2048]{2,1,0:T(8,128)(2,1)} async-done(((bf16[1,2048,128]{2,1,0:T(8,128)(2,1)}), bf16[1,2048,2048]{2,1,0:T(8,128)(2,1)}) %all-gather.11.cloned.1.call-update) | async-done | bytes 8388624 | tf_op jit(solution)/shard_map/all_gather | solution.py:39
  138.0 6.3 %fusion.2 = f32[128,2048]{1,0:T(8,128)S(1)} fusion(f32[2048,128]{1,0:T(8,128)S(1)} %convolution_subtract_fusion.1, bf16[1,2048,2048]{2,1,0:T(8,128)(2,1)} %all-gather.11.cloned.1.call-done), kind=kOutput, calls=%fused_computation.6 | convolution fusion | flops 6442450944 | bytes 10485760 | tf_op jit(solution)/shard_map/dot_general | solution.py:38
  144.6 27.9 %gather_fusion.1 = f32[8192,128]{1,0:T(8,128)} fusion(f32[2048,128]{1,0:T(8,128)S(1)} %copy.21, s32[8192]{0:T(1024)S(1)} %broadcast_clamp_fusion), kind=kCustom, calls=%fused_computation.3 | custom fusion | bytes 8421376 | tf_op jit(solution)/shard_map/jit(_take)/gather | solution.py:70
  172.5 3.6 select_multiply_fusion
  176.1 56.9 %all_to_all.5 = f32[16,512,128]{2,1,0:T(8,128)} all-to-all(f32[16,512,128]{2,1,0:T(8,128)S(1)} %select_multiply_fusion), channel_id=1, replica_groups=mesh['leaf'=16,'row'=16] {'leaf'}, dimensions={0} | all-to-all | bytes 8388608 | tf_op jit(solution)/shard_map/all_to_all | solution.py:72
  233.0 2.5 reduce_sum.9
  235.5 0.8 copy.22
  237.1 3.3 collective-permute-start.15
  240.4 1.9 collective-permute-done.15
  242.4 2.4 collective-permute-start.16
  244.8 3.6 collective-permute-done.16
  248.5 2.5 collective-permute-start.17
  250.9 4.2 %collective-permute-done.17 = bf16[512,128]{1,0:T(8,128)(2,1)S(1)} collective-permute-done((bf16[512,128]{1,0:T(8,128)(2,1)S(1)}, bf16[512,128]{1,0:T(8,128)(2,1)S(1)}, u32[]{:S(2)}, u32[]{:S(2)}) %collective-permute-start.17) | collective-permute-done | bytes 131104 | tf_op jit(solution)/shard_map/ppermute | solution.py:29
  255.2 2.5 collective-permute-start.18
  257.7 4.2 %collective-permute-done.18 = bf16[512,128]{1,0:T(8,128)(2,1)S(1)} collective-permute-done((bf16[512,128]{1,0:T(8,128)(2,1)S(1)}, bf16[512,128]{1,0:T(8,128)(2,1)S(1)}, u32[]{:S(2)}, u32[]{:S(2)}) %collective-permute-start.18) | collective-permute-done | bytes 131104 | tf_op jit(solution)/shard_map/ppermute | solution.py:29
  261.9 2.5 collective-permute-start.19
  264.3 5.0 %collective-permute-done.19 = bf16[512,128]{1,0:T(8,128)(2,1)S(1)} collective-permute-done((bf16[512,128]{1,0:T(8,128)(2,1)S(1)}, bf16[512,128]{1,0:T(8,128)(2,1)S(1)}, u32[]{:S(2)}, u32[]{:S(2)}) %collective-permute-start.19) | collective-permute-done | bytes 131104 | tf_op jit(solution)/shard_map/ppermute | solution.py:29
  269.3 0.9 collective-permute-start.20
  270.2 6.0 %collective-permute-done.20 = bf16[512,128]{1,0:T(8,128)(2,1)S(1)} collective-permute-done((bf16[512,128]{1,0:T(8,128)(2,1)S(1)}, bf16[512,128]{1,0:T(8,128)(2,1)S(1)}, u32[]{:S(2)}, u32[]{:S(2)}) %collective-permute-start.20) | collective-permute-done | bytes 131104 | tf_op jit(solution)/shard_map/ppermute | solution.py:29
  276.2 5.6 %collective-permute-done.21 = bf16[512,128]{1,0:T(8,128)(2,1)S(1)} collective-permute-done((bf16[512,128]{1,0:T(8,128)(2,1)S(1)}, bf16[512,128]{1,0:T(8,128)(2,1)S(1)}, u32[]{:S(2)}, u32[]{:S(2)}) %collective-permute-start.21) | collective-permute-done | bytes 131104 | tf_op jit(solution)/shard_map/ppermute | solution.py:29
  281.8 5.6 %collective-permute-done.22 = bf16[512,128]{1,0:T(8,128)(2,1)S(1)} collective-permute-done((bf16[512,128]{1,0:T(8,128)(2,1)S(1)}, bf16[512,128]{1,0:T(8,128)(2,1)S(1)}, u32[]{:S(2)}, u32[]{:S(2)}) %collective-permute-start.22) | collective-permute-done | bytes 131104 | tf_op jit(solution)/shard_map/ppermute | solution.py:29
  287.4 5.6 %collective-permute-done.23 = bf16[512,128]{1,0:T(8,128)(2,1)S(1)} collective-permute-done((bf16[512,128]{1,0:T(8,128)(2,1)S(1)}, bf16[512,128]{1,0:T(8,128)(2,1)S(1)}, u32[]{:S(2)}, u32[]{:S(2)}) %collective-permute-start.23) | collective-permute-done | bytes 131104 | tf_op jit(solution)/shard_map/ppermute | solution.py:29
  293.3 7.4 %collective-permute-done.24 = bf16[512,128]{1,0:T(8,128)(2,1)S(1)} collective-permute-done((bf16[512,128]{1,0:T(8,128)(2,1)S(1)}, bf16[512,128]{1,0:T(8,128)(2,1)S(1)}, u32[]{:S(2)}, u32[]{:S(2)}) %collective-permute-start.24) | collective-permute-done | bytes 131104 | tf_op jit(solution)/shard_map/ppermute | solution.py:29
  300.7 8.2 %collective-permute-done.25 = bf16[512,128]{1,0:T(8,128)(2,1)S(1)} collective-permute-done((bf16[512,128]{1,0:T(8,128)(2,1)S(1)}, bf16[512,128]{1,0:T(8,128)(2,1)S(1)}, u32[]{:S(2)}, u32[]{:S(2)}) %collective-permute-start.25) | collective-permute-done | bytes 131104 | tf_op jit(solution)/shard_map/ppermute | solution.py:29
  309.0 8.2 %collective-permute-done.26 = bf16[512,128]{1,0:T(8,128)(2,1)S(1)} collective-permute-done((bf16[512,128]{1,0:T(8,128)(2,1)S(1)}, bf16[512,128]{1,0:T(8,128)(2,1)S(1)}, u32[]{:S(2)}, u32[]{:S(2)}) %collective-permute-start.26) | collective-permute-done | bytes 131104 | tf_op jit(solution)/shard_map/ppermute | solution.py:29
  317.2 8.3 %collective-permute-done.27 = bf16[512,128]{1,0:T(8,128)(2,1)S(1)} collective-permute-done((bf16[512,128]{1,0:T(8,128)(2,1)S(1)}, bf16[512,128]{1,0:T(8,128)(2,1)S(1)}, u32[]{:S(2)}, u32[]{:S(2)}) %collective-permute-start.27) | collective-permute-done | bytes 131104 | tf_op jit(solution)/shard_map/ppermute | solution.py:29
  325.5 8.0 %collective-permute-done.28 = bf16[512,128]{1,0:T(8,128)(2,1)S(1)} collective-permute-done((bf16[512,128]{1,0:T(8,128)(2,1)S(1)}, bf16[512,128]{1,0:T(8,128)(2,1)S(1)}, u32[]{:S(2)}, u32[]{:S(2)}) %collective-permute-start.28) | collective-permute-done | bytes 131104 | tf_op jit(solution)/shard_map/ppermute | solution.py:29
  333.6 8.1 %collective-permute-done.29 = bf16[512,128]{1,0:T(8,128)(2,1)S(1)} collective-permute-done((bf16[512,128]{1,0:T(8,128)(2,1)S(1)}, bf16[512,128]{1,0:T(8,128)(2,1)S(1)}, u32[]{:S(2)}, u32[]{:S(2)}) %collective-permute-start.29) | collective-permute-done | bytes 131104 | tf_op jit(solution)/shard_map/ppermute | solution.py:29
  342.5 1.9 fusion.13
  344.5 1.3 copy.23
  345.8 4.3 %gather_fusion.3 = f32[512,512]{1,0:T(8,128)S(1)} fusion(f32[512,2048]{0,1:T(8,128)} %all-gather.9.cloned.1.call-done, s32[1024]{0:T(1024)S(1)} %pad_clamp_fusion), kind=kCustom, calls=%fused_computation.1.clone | custom fusion | bytes 2099200 | tf_op jit(solution)/shard_map/jit(_take)/gather | solution.py:20
  350.1 1.9 convolution_negate_fusion
  352.1 4.4 %convolution_subtract_fusion = f32[2048,128]{1,0:T(8,128)S(1)} fusion(f32[512,128]{1,0:T(8,128)S(1)} %convolution_negate_fusion, bf16[1,2048,128]{2,1,0:T(8,128)(2,1)} %param.19, s32[]{:T(128)S(6)} %select_n.78, bf16[512,2048]{1,0:T(8,128)(2,1)} %copy-done.9), kind=kOutput, calls=%fused_computation.14 | convolution fusion | flops 1615331328 | bytes 3932164 | tf_op jit(solution)/shard_map/dot_general | solution.py:35
  356.5 6.3 %fusion.4 = f32[1,2048,128]{1,2,0:T(8,128)S(1)} fusion(f32[2048,128]{1,0:T(8,128)S(1)} %convolution_subtract_fusion, bf16[1,2048,2048]{2,1,0:T(8,128)(2,1)} %all-gather.13.cloned.1.call-done), kind=kOutput, calls=%fused_computation.13 | convolution fusion | flops 6442450944 | bytes 10485760 | tf_op jit(solution)/shard_map/dot_general | solution.py:38
  362.8 1.3 copy.24
  (117 shorter events, 5.4 us)
Async XLA Ops:
  7.2 1.2 copy-start
  7.2 3.9 %copy-start.11 = (s32[1,4,1]{1,2,0:T(1,128)S(1)}, s32[1,4,1]{1,2,0:T(1,128)}, u32[]{:S(2)}) copy-start(s32[1,4,1]{1,2,0:T(1,128)} %param.18) | copy-start | bytes 52
  7.2 4.0 %copy-start.3 = (bf16[1,512,128]{2,1,0:T(8,128)(2,1)S(1)}, bf16[1,512,128]{2,1,0:T(8,128)(2,1)}, u32[]{:S(2)}) copy-start(bf16[1,512,128]{2,1,0:T(8,128)(2,1)} %param.16) | copy-start | bytes 393220
  7.2 52.9 %copy-start.10 = (s32[16,4]{0,1:T(4,128)S(1)}, s32[16,4]{0,1:T(4,128)}, u32[]{:S(2)}) copy-start(s32[16,4]{0,1:T(4,128)} %param.21) | copy-start | bytes 772
  7.2 106.2 %all-gather.7.cloned.1.call-start = ((), (), s32[]{:S(2)}) async-start(), calls=%async_computation.1 | async-start | bytes 4456448 | tf_op jit(solution)/shard_map/all_gather | solution.py:19
  8.4 91.2 %copy-start.12 = (s32[16]{0:T(128)S(1)}, s32[16]{0:T(128)}, u32[]{:S(2)}) copy-start(s32[16]{0:T(128)} %param.23) | copy-start | bytes 196
  10.3 127.7 %all-gather.11.cloned.1.call-start = ((), (), s32[]{:S(2)}) async-start(), calls=%async_computation.3 | async-start | bytes 8912896 | tf_op jit(solution)/shard_map/all_gather | solution.py:39
  11.1 334.7 %all-gather.9.cloned.1.call-start = ((), (), s32[]{:S(2)}) async-start(), calls=%async_computation.2 | async-start | bytes 4456448 | tf_op jit(solution)/shard_map/all_gather | solution.py:19
  11.3 5.0 %collective-permute-start = (bf16[512,128]{1,0:T(8,128)(2,1)S(1)}, bf16[512,128]{1,0:T(8,128)(2,1)S(1)}, u32[]{:S(2)}, u32[]{:S(2)}) collective-permute-start(bf16[512,128]{1,0:T(8,128)(2,1)S(1)} %bitcast_multiply_fusion.1), channel_id=1, source_target_pairs={{0,1},{1,2},{2,3},{3,4},{4,5},{5,6},{6,7},{7,8},{8,9},{9,10},{10,1... | collective-permute-start | bytes 393224 | tf_op jit(solution)/shard_map/ppermute | solution.py:29
  16.3 5.3 %collective-permute-start.1 = (bf16[512,128]{1,0:T(8,128)(2,1)S(1)}, bf16[512,128]{1,0:T(8,128)(2,1)S(1)}, u32[]{:S(2)}, u32[]{:S(2)}) collective-permute-start(bf16[512,128]{1,0:T(8,128)(2,1)S(1)} %collective-permute-done), channel_id=1, source_target_pairs={{0,1},{1,2},{2,3},{3,4},{4,5},{5,6},{6,7},{7,8},{8,9},{9,10},{10,1... | collective-permute-start | bytes 393224 | tf_op jit(solution)/shard_map/ppermute | solution.py:29
  21.7 5.6 %collective-permute-start.2 = (bf16[512,128]{1,0:T(8,128)(2,1)S(1)}, bf16[512,128]{1,0:T(8,128)(2,1)S(1)}, u32[]{:S(2)}, u32[]{:S(2)}) collective-permute-start(bf16[512,128]{1,0:T(8,128)(2,1)S(1)} %collective-permute-done.1), channel_id=1, source_target_pairs={{0,1},{1,2},{2,3},{3,4},{4,5},{5,6},{6,7},{7,8},{8,9},{9,10},{10,1... | collective-permute-start | bytes 393224 | tf_op jit(solution)/shard_map/ppermute | solution.py:29
  27.3 7.7 %collective-permute-start.3 = (bf16[512,128]{1,0:T(8,128)(2,1)S(1)}, bf16[512,128]{1,0:T(8,128)(2,1)S(1)}, u32[]{:S(2)}, u32[]{:S(2)}) collective-permute-start(bf16[512,128]{1,0:T(8,128)(2,1)S(1)} %collective-permute-done.2), channel_id=1, source_target_pairs={{0,1},{1,2},{2,3},{3,4},{4,5},{5,6},{6,7},{7,8},{8,9},{9,10},{10,1... | collective-permute-start | bytes 393224 | tf_op jit(solution)/shard_map/ppermute | solution.py:29
  34.9 6.1 %collective-permute-start.4 = (bf16[512,128]{1,0:T(8,128)(2,1)S(1)}, bf16[512,128]{1,0:T(8,128)(2,1)S(1)}, u32[]{:S(2)}, u32[]{:S(2)}) collective-permute-start(bf16[512,128]{1,0:T(8,128)(2,1)S(1)} %collective-permute-done.3), channel_id=1, source_target_pairs={{0,1},{1,2},{2,3},{3,4},{4,5},{5,6},{6,7},{7,8},{8,9},{9,10},{10,1... | collective-permute-start | bytes 393224 | tf_op jit(solution)/shard_map/ppermute | solution.py:29
  41.0 5.7 %collective-permute-start.5 = (bf16[512,128]{1,0:T(8,128)(2,1)S(1)}, bf16[512,128]{1,0:T(8,128)(2,1)S(1)}, u32[]{:S(2)}, u32[]{:S(2)}) collective-permute-start(bf16[512,128]{1,0:T(8,128)(2,1)S(1)} %collective-permute-done.4), channel_id=1, source_target_pairs={{0,1},{1,2},{2,3},{3,4},{4,5},{5,6},{6,7},{7,8},{8,9},{9,10},{10,1... | collective-permute-start | bytes 393224 | tf_op jit(solution)/shard_map/ppermute | solution.py:29
  46.7 6.8 %collective-permute-start.6 = (bf16[512,128]{1,0:T(8,128)(2,1)S(1)}, bf16[512,128]{1,0:T(8,128)(2,1)S(1)}, u32[]{:S(2)}, u32[]{:S(2)}) collective-permute-start(bf16[512,128]{1,0:T(8,128)(2,1)S(1)} %collective-permute-done.5), channel_id=1, source_target_pairs={{0,1},{1,2},{2,3},{3,4},{4,5},{5,6},{6,7},{7,8},{8,9},{9,10},{10,1... | collective-permute-start | bytes 393224 | tf_op jit(solution)/shard_map/ppermute | solution.py:29
  53.5 6.2 %collective-permute-start.7 = (bf16[512,128]{1,0:T(8,128)(2,1)S(1)}, bf16[512,128]{1,0:T(8,128)(2,1)S(1)}, u32[]{:S(2)}, u32[]{:S(2)}) collective-permute-start(bf16[512,128]{1,0:T(8,128)(2,1)S(1)} %collective-permute-done.6), channel_id=1, source_target_pairs={{0,1},{1,2},{2,3},{3,4},{4,5},{5,6},{6,7},{7,8},{8,9},{9,10},{10,1... | collective-permute-start | bytes 393224 | tf_op jit(solution)/shard_map/ppermute | solution.py:29
  59.6 6.6 %collective-permute-start.8 = (bf16[512,128]{1,0:T(8,128)(2,1)S(1)}, bf16[512,128]{1,0:T(8,128)(2,1)S(1)}, u32[]{:S(2)}, u32[]{:S(2)}) collective-permute-start(bf16[512,128]{1,0:T(8,128)(2,1)S(1)} %collective-permute-done.7), channel_id=1, source_target_pairs={{0,1},{1,2},{2,3},{3,4},{4,5},{5,6},{6,7},{7,8},{8,9},{9,10},{10,1... | collective-permute-start | bytes 393224 | tf_op jit(solution)/shard_map/ppermute | solution.py:29
  66.2 5.6 %collective-permute-start.9 = (bf16[512,128]{1,0:T(8,128)(2,1)S(1)}, bf16[512,128]{1,0:T(8,128)(2,1)S(1)}, u32[]{:S(2)}, u32[]{:S(2)}) collective-permute-start(bf16[512,128]{1,0:T(8,128)(2,1)S(1)} %collective-permute-done.8), channel_id=1, source_target_pairs={{0,1},{1,2},{2,3},{3,4},{4,5},{5,6},{6,7},{7,8},{8,9},{9,10},{10,1... | collective-permute-start | bytes 393224 | tf_op jit(solution)/shard_map/ppermute | solution.py:29
  71.8 5.6 %collective-permute-start.10 = (bf16[512,128]{1,0:T(8,128)(2,1)S(1)}, bf16[512,128]{1,0:T(8,128)(2,1)S(1)}, u32[]{:S(2)}, u32[]{:S(2)}) collective-permute-start(bf16[512,128]{1,0:T(8,128)(2,1)S(1)} %collective-permute-done.9), channel_id=1, source_target_pairs={{0,1},{1,2},{2,3},{3,4},{4,5},{5,6},{6,7},{7,8},{8,9},{9,10},{10,1... | collective-permute-start | bytes 393224 | tf_op jit(solution)/shard_map/ppermute | solution.py:29
  77.4 5.6 %collective-permute-start.11 = (bf16[512,128]{1,0:T(8,128)(2,1)S(1)}, bf16[512,128]{1,0:T(8,128)(2,1)S(1)}, u32[]{:S(2)}, u32[]{:S(2)}) collective-permute-start(bf16[512,128]{1,0:T(8,128)(2,1)S(1)} %collective-permute-done.10), channel_id=1, source_target_pairs={{0,1},{1,2},{2,3},{3,4},{4,5},{5,6},{6,7},{7,8},{8,9},{9,10},{10,1... | collective-permute-start | bytes 393224 | tf_op jit(solution)/shard_map/ppermute | solution.py:29
  83.0 8.3 %collective-permute-start.12 = (bf16[512,128]{1,0:T(8,128)(2,1)S(1)}, bf16[512,128]{1,0:T(8,128)(2,1)S(1)}, u32[]{:S(2)}, u32[]{:S(2)}) collective-permute-start(bf16[512,128]{1,0:T(8,128)(2,1)S(1)} %collective-permute-done.11), channel_id=1, source_target_pairs={{0,1},{1,2},{2,3},{3,4},{4,5},{5,6},{6,7},{7,8},{8,9},{9,10},{10,1... | collective-permute-start | bytes 393224 | tf_op jit(solution)/shard_map/ppermute | solution.py:29
  91.3 8.3 %collective-permute-start.13 = (bf16[512,128]{1,0:T(8,128)(2,1)S(1)}, bf16[512,128]{1,0:T(8,128)(2,1)}, u32[]{:S(2)}, u32[]{:S(2)}) collective-permute-start(bf16[512,128]{1,0:T(8,128)(2,1)S(1)} %collective-permute-done.12), channel_id=1, source_target_pairs={{0,1},{1,2},{2,3},{3,4},{4,5},{5,6},{6,7},{7,8},{8,9},{9,10},{10,1... | collective-permute-start | bytes 393224 | tf_op jit(solution)/shard_map/ppermute | solution.py:29
  99.6 8.6 %collective-permute-start.14 = (bf16[512,128]{1,0:T(8,128)(2,1)}, bf16[512,128]{1,0:T(8,128)(2,1)}, u32[]{:S(2)}, u32[]{:S(2)}) collective-permute-start(bf16[512,128]{1,0:T(8,128)(2,1)} %collective-permute-done.13), channel_id=1, source_target_pairs={{0,1},{1,2},{2,3},{3,4},{4,5},{5,6},{6,7},{7,8},{8,9},{9,10},{10,1... | collective-permute-start | bytes 393224 | tf_op jit(solution)/shard_map/ppermute | solution.py:29
  99.7 12.5 %copy-start.1 = (bf16[1,2048,128]{2,1,0:T(8,128)(2,1)S(1)}, bf16[1,2048,128]{2,1,0:T(8,128)(2,1)}, u32[]{:S(2)}) copy-start(bf16[1,2048,128]{2,1,0:T(8,128)(2,1)} %param.15) | copy-start | bytes 1572868
  110.8 1.3 copy-start.8
  125.0 4.3 %copy-start.5 = (f32[512,128]{1,0:T(8,128)}, f32[512,128]{1,0:T(8,128)S(1)}, u32[]{:S(2)}) copy-start(f32[512,128]{1,0:T(8,128)S(1)} %convolution_negate_fusion.1) | copy-start | bytes 786436
  233.0 3.9 %copy-start.13 = (s32[1,4,1]{1,2,0:T(1,128)S(1)}, s32[1,4,1]{1,2,0:T(1,128)}, u32[]{:S(2)}) copy-start(s32[1,4,1]{1,2,0:T(1,128)} %param.22) | copy-start | bytes 52
  233.0 4.0 %copy-start.4 = (bf16[1,512,128]{2,1,0:T(8,128)(2,1)S(1)}, bf16[1,512,128]{2,1,0:T(8,128)(2,1)}, u32[]{:S(2)}) copy-start(bf16[1,512,128]{2,1,0:T(8,128)(2,1)} %param.20) | copy-start | bytes 393220
  236.3 120.2 %all-gather.13.cloned.1.call-start = ((), (), s32[]{:S(2)}) async-start(), calls=%async_computation.4 | async-start | bytes 8912896 | tf_op jit(solution)/shard_map/all_gather | solution.py:39
  237.1 5.2 %collective-permute-start.15 = (bf16[512,128]{1,0:T(8,128)(2,1)S(1)}, bf16[512,128]{1,0:T(8,128)(2,1)S(1)}, u32[]{:S(2)}, u32[]{:S(2)}) collective-permute-start(bf16[512,128]{1,0:T(8,128)(2,1)S(1)} %bitcast_multiply_fusion), channel_id=1, source_target_pairs={{0,1},{1,2},{2,3},{3,4},{4,5},{5,6},{6,7},{7,8},{8,9},{9,10},{10,1... | collective-permute-start | bytes 393224 | tf_op jit(solution)/shard_map/ppermute | solution.py:29
  242.4 6.1 %collective-permute-start.16 = (bf16[512,128]{1,0:T(8,128)(2,1)S(1)}, bf16[512,128]{1,0:T(8,128)(2,1)S(1)}, u32[]{:S(2)}, u32[]{:S(2)}) collective-permute-start(bf16[512,128]{1,0:T(8,128)(2,1)S(1)} %collective-permute-done.15), channel_id=1, source_target_pairs={{0,1},{1,2},{2,3},{3,4},{4,5},{5,6},{6,7},{7,8},{8,9},{9,10},{10,1... | collective-permute-start | bytes 393224 | tf_op jit(solution)/shard_map/ppermute | solution.py:29
  248.5 6.7 %collective-permute-start.17 = (bf16[512,128]{1,0:T(8,128)(2,1)S(1)}, bf16[512,128]{1,0:T(8,128)(2,1)S(1)}, u32[]{:S(2)}, u32[]{:S(2)}) collective-permute-start(bf16[512,128]{1,0:T(8,128)(2,1)S(1)} %collective-permute-done.16), channel_id=1, source_target_pairs={{0,1},{1,2},{2,3},{3,4},{4,5},{5,6},{6,7},{7,8},{8,9},{9,10},{10,1... | collective-permute-start | bytes 393224 | tf_op jit(solution)/shard_map/ppermute | solution.py:29
  255.2 6.7 %collective-permute-start.18 = (bf16[512,128]{1,0:T(8,128)(2,1)S(1)}, bf16[512,128]{1,0:T(8,128)(2,1)S(1)}, u32[]{:S(2)}, u32[]{:S(2)}) collective-permute-start(bf16[512,128]{1,0:T(8,128)(2,1)S(1)} %collective-permute-done.17), channel_id=1, source_target_pairs={{0,1},{1,2},{2,3},{3,4},{4,5},{5,6},{6,7},{7,8},{8,9},{9,10},{10,1... | collective-permute-start | bytes 393224 | tf_op jit(solution)/shard_map/ppermute | solution.py:29
  261.9 7.4 %collective-permute-start.19 = (bf16[512,128]{1,0:T(8,128)(2,1)S(1)}, bf16[512,128]{1,0:T(8,128)(2,1)S(1)}, u32[]{:S(2)}, u32[]{:S(2)}) collective-permute-start(bf16[512,128]{1,0:T(8,128)(2,1)S(1)} %collective-permute-done.18), channel_id=1, source_target_pairs={{0,1},{1,2},{2,3},{3,4},{4,5},{5,6},{6,7},{7,8},{8,9},{9,10},{10,1... | collective-permute-start | bytes 393224 | tf_op jit(solution)/shard_map/ppermute | solution.py:29
  269.3 6.9 %collective-permute-start.20 = (bf16[512,128]{1,0:T(8,128)(2,1)S(1)}, bf16[512,128]{1,0:T(8,128)(2,1)S(1)}, u32[]{:S(2)}, u32[]{:S(2)}) collective-permute-start(bf16[512,128]{1,0:T(8,128)(2,1)S(1)} %collective-permute-done.19), channel_id=1, source_target_pairs={{0,1},{1,2},{2,3},{3,4},{4,5},{5,6},{6,7},{7,8},{8,9},{9,10},{10,1... | collective-permute-start | bytes 393224 | tf_op jit(solution)/shard_map/ppermute | solution.py:29
  276.2 5.6 %collective-permute-start.21 = (bf16[512,128]{1,0:T(8,128)(2,1)S(1)}, bf16[512,128]{1,0:T(8,128)(2,1)S(1)}, u32[]{:S(2)}, u32[]{:S(2)}) collective-permute-start(bf16[512,128]{1,0:T(8,128)(2,1)S(1)} %collective-permute-done.20), channel_id=1, source_target_pairs={{0,1},{1,2},{2,3},{3,4},{4,5},{5,6},{6,7},{7,8},{8,9},{9,10},{10,1... | collective-permute-start | bytes 393224 | tf_op jit(solution)/shard_map/ppermute | solution.py:29
  281.8 5.6 %collective-permute-start.22 = (bf16[512,128]{1,0:T(8,128)(2,1)S(1)}, bf16[512,128]{1,0:T(8,128)(2,1)S(1)}, u32[]{:S(2)}, u32[]{:S(2)}) collective-permute-start(bf16[512,128]{1,0:T(8,128)(2,1)S(1)} %collective-permute-done.21), channel_id=1, source_target_pairs={{0,1},{1,2},{2,3},{3,4},{4,5},{5,6},{6,7},{7,8},{8,9},{9,10},{10,1... | collective-permute-start | bytes 393224 | tf_op jit(solution)/shard_map/ppermute | solution.py:29
  287.4 5.6 %collective-permute-start.23 = (bf16[512,128]{1,0:T(8,128)(2,1)S(1)}, bf16[512,128]{1,0:T(8,128)(2,1)S(1)}, u32[]{:S(2)}, u32[]{:S(2)}) collective-permute-start(bf16[512,128]{1,0:T(8,128)(2,1)S(1)} %collective-permute-done.22), channel_id=1, source_target_pairs={{0,1},{1,2},{2,3},{3,4},{4,5},{5,6},{6,7},{7,8},{8,9},{9,10},{10,1... | collective-permute-start | bytes 393224 | tf_op jit(solution)/shard_map/ppermute | solution.py:29
  293.0 7.7 %collective-permute-start.24 = (bf16[512,128]{1,0:T(8,128)(2,1)S(1)}, bf16[512,128]{1,0:T(8,128)(2,1)S(1)}, u32[]{:S(2)}, u32[]{:S(2)}) collective-permute-start(bf16[512,128]{1,0:T(8,128)(2,1)S(1)} %collective-permute-done.23), channel_id=1, source_target_pairs={{0,1},{1,2},{2,3},{3,4},{4,5},{5,6},{6,7},{7,8},{8,9},{9,10},{10,1... | collective-permute-start | bytes 393224 | tf_op jit(solution)/shard_map/ppermute | solution.py:29
  300.7 8.2 %collective-permute-start.25 = (bf16[512,128]{1,0:T(8,128)(2,1)S(1)}, bf16[512,128]{1,0:T(8,128)(2,1)S(1)}, u32[]{:S(2)}, u32[]{:S(2)}) collective-permute-start(bf16[512,128]{1,0:T(8,128)(2,1)S(1)} %collective-permute-done.24), channel_id=1, source_target_pairs={{0,1},{1,2},{2,3},{3,4},{4,5},{5,6},{6,7},{7,8},{8,9},{9,10},{10,1... | collective-permute-start | bytes 393224 | tf_op jit(solution)/shard_map/ppermute | solution.py:29
  308.9 8.3 %collective-permute-start.26 = (bf16[512,128]{1,0:T(8,128)(2,1)S(1)}, bf16[512,128]{1,0:T(8,128)(2,1)S(1)}, u32[]{:S(2)}, u32[]{:S(2)}) collective-permute-start(bf16[512,128]{1,0:T(8,128)(2,1)S(1)} %collective-permute-done.25), channel_id=1, source_target_pairs={{0,1},{1,2},{2,3},{3,4},{4,5},{5,6},{6,7},{7,8},{8,9},{9,10},{10,1... | collective-permute-start | bytes 393224 | tf_op jit(solution)/shard_map/ppermute | solution.py:29
  317.2 8.3 %collective-permute-start.27 = (bf16[512,128]{1,0:T(8,128)(2,1)S(1)}, bf16[512,128]{1,0:T(8,128)(2,1)S(1)}, u32[]{:S(2)}, u32[]{:S(2)}) collective-permute-start(bf16[512,128]{1,0:T(8,128)(2,1)S(1)} %collective-permute-done.26), channel_id=1, source_target_pairs={{0,1},{1,2},{2,3},{3,4},{4,5},{5,6},{6,7},{7,8},{8,9},{9,10},{10,1... | collective-permute-start | bytes 393224 | tf_op jit(solution)/shard_map/ppermute | solution.py:29
  325.5 8.0 %collective-permute-start.28 = (bf16[512,128]{1,0:T(8,128)(2,1)S(1)}, bf16[512,128]{1,0:T(8,128)(2,1)S(1)}, u32[]{:S(2)}, u32[]{:S(2)}) collective-permute-start(bf16[512,128]{1,0:T(8,128)(2,1)S(1)} %collective-permute-done.27), channel_id=1, source_target_pairs={{0,1},{1,2},{2,3},{3,4},{4,5},{5,6},{6,7},{7,8},{8,9},{9,10},{10,1... | collective-permute-start | bytes 393224 | tf_op jit(solution)/shard_map/ppermute | solution.py:29
  333.5 8.1 %collective-permute-start.29 = (bf16[512,128]{1,0:T(8,128)(2,1)S(1)}, bf16[512,128]{1,0:T(8,128)(2,1)S(1)}, u32[]{:S(2)}, u32[]{:S(2)}) collective-permute-start(bf16[512,128]{1,0:T(8,128)(2,1)S(1)} %collective-permute-done.28), channel_id=1, source_target_pairs={{0,1},{1,2},{2,3},{3,4},{4,5},{5,6},{6,7},{7,8},{8,9},{9,10},{10,1... | collective-permute-start | bytes 393224 | tf_op jit(solution)/shard_map/ppermute | solution.py:29
  333.6 9.0 %copy-start.2 = (bf16[1,2048,128]{2,1,0:T(8,128)(2,1)S(1)}, bf16[1,2048,128]{2,1,0:T(8,128)(2,1)}, u32[]{:S(2)}) copy-start(bf16[1,2048,128]{2,1,0:T(8,128)(2,1)} %param.19) | copy-start | bytes 1572868
  342.5 1.9 copy-start.9
  345.8 4.4 %copy-start.7 = (f32[512,128]{1,0:T(8,128)S(1)}, f32[512,128]{1,0:T(8,128)}, u32[]{:S(2)}) copy-start(f32[512,128]{1,0:T(8,128)} %fusion.13) | copy-start | bytes 786436
  352.0 4.4 %copy-start.6 = (f32[512,128]{1,0:T(8,128)}, f32[512,128]{1,0:T(8,128)S(1)}, u32[]{:S(2)}) copy-start(f32[512,128]{1,0:T(8,128)S(1)} %convolution_negate_fusion) | copy-start | bytes 786436
Sparse Core Ops, SparseCore 0:
  10.4 56.9 all-gather.6
  69.2 68.8 all-gather.10
  236.4 40.8 all-gather.8
  279.0 72.8 all-gather.12
